TPU v7x, 128 devices: a whole 4x4x4 slice. The times are simulated.
128 devices in a mesh: chan: 8 (over x, core), row: 16 (over y, z).
Axes of the slice: x: 4, y: 4, z: 4, core: 2. Of those that a mesh axis runs over, the one named last changes fastest.
Arguments:
- generator: bfloat16 [8, 2560, 2560], P('chan', 'row'), may hold values from -0.06 to 0.06, as said below
- hamiltonian: bfloat16 [8, 2560, 2560], P('chan', 'row'), may hold values from -6 to 6, as said below
- live_states: int32 [8], P('chan'), may hold values from 1 to 2560, 11520 in all
- pp_occupation: int32 [8, 2560], P('chan'), may hold values from -1 to 1
- ph_occupation: int32 [8, 2560], P('chan'), may hold values from -1 to 1
- ph_order: int32 [8, 2560], P('chan'), may hold values from 0 to 2559, as said below
- recoupling: float32 [8, 2], replicated, may hold values from 0.4 to 1
Outputs:
- transformed: float32 [8, 2560, 2560], P('chan', 'row')
Inputs may be any that keep to these rules, and one draw needn't show every extreme that they name: Each generator[c] is antisymmetric. Each hamiltonian[c] is symmetric. Each ph_order[c] is a permutation of 0 to 2559, and entry r * 160 + q * 16 + s, for 0 <= q < 10, lies in [s * 160, (s + 1) * 160).
All inputs are finite; a program needn't handle non-finite values. No bound on the sum of `live_states` on one device may be relied on, other than what follows from the above.
Results may differ from a plain program's by a relative error of at most 0.005.
Values may be sent and summed in bfloat16 or wider, within the bound.
No kernel may reach another device: no remote copies, remote signals or barrier semaphores. Data moves between devices by JAX's collectives and lax.ppermute only.
A program may use at most 128 MiB of HBM per device.

v0:
```python
import jax
import jax.numpy as jnp
from jax import lax
from jax.sharding import Mesh, PartitionSpec as P

TERMS = 3


def swapped(value):
    return lax.ppermute(value, "hi", [(0, 1), (1, 0)])


def on_device(
    generator, hamiltonian, live_states, pp_occupation, ph_occupation, ph_order, recoupling
):
    row_count = generator.shape[1]
    state_count = generator.shape[2]
    half = row_count // 2
    shard_count = lax.axis_size("row")
    hi = lax.axis_index("hi")
    lo = lax.axis_index("lo")
    my_shard = lax.axis_index("row")
    first = hi == 0
    r0 = recoupling[lo]
    r1 = recoupling[lo + lax.axis_size("lo")]
    positions = jnp.arange(state_count, dtype=jnp.int32)
    live_count = live_states[0]
    column_alive = positions < live_count
    row_alive = my_shard * row_count + jnp.arange(row_count, dtype=jnp.int32) < live_count
    block_alive = row_alive[:, None] & column_alive[None, :]
    own_share = jnp.where(block_alive, generator[0], jnp.zeros_like(generator[0]))
    far_share = swapped(own_share)
    full_own = lax.all_gather(own_share, "row", axis=0, tiled=True)
    full_far = lax.all_gather(far_share, "row", axis=0, tiled=True)
    pp = jnp.where(column_alive, pp_occupation[0], 0)
    ph = jnp.zeros((state_count,), jnp.int32).at[ph_order[0]].set(ph_occupation[0])
    ph = jnp.where(column_alive, ph, 0)
    mine = jnp.stack([pp, ph]).astype(jnp.float32)
    other = swapped(mine)
    d0, n0 = jnp.where(first, mine, other)
    d1, n1 = jnp.where(first, other, mine)
    a0 = d0 + r0[0] ** 3 * n0 + r1[1] ** 3 * n1
    a1 = d1 + r1[0] ** 3 * n1 + r0[1] ** 3 * n0
    p = r0[0] ** 2 * r0[1] * n0 + r1[1] ** 2 * r1[0] * n1
    q = r1[0] ** 2 * r1[1] * n1 + r0[1] ** 2 * r0[0] * n0
    zero_set = jnp.stack([a0, p, p, q])
    one_set = jnp.stack([p, q, q, a1])
    own_set = jnp.where(first, zero_set, one_set)
    far_set = jnp.where(first, one_set, zero_set)
    own_ham = jnp.where(block_alive, hamiltonian[0], jnp.zeros_like(hamiltonian[0]))
    keep = lax.dynamic_slice_in_dim(own_ham, hi * half, half, 0)
    gone = lax.dynamic_slice_in_dim(own_ham, (1 - hi) * half, half, 0)
    came = swapped(gone)
    current = jnp.concatenate([jnp.where(first, keep, came), jnp.where(first, came, keep)])
    running = jnp.zeros(current.shape, jnp.float32)

    def mix(x, s):
        x0, x1 = (x[:half], x[half:])
        top = x0 * s[0] + x1 * s[1]
        low = x0 * s[2] + x1 * s[3]
        return jnp.concatenate([top, low]).astype(jnp.bfloat16)

    for term_index in range(1, TERMS + 1):
        wide = current.astype(jnp.float32)
        combined = jnp.dot(
            mix(wide, own_set), full_own, preferred_element_type=jnp.float32
        ) + jnp.dot(mix(wide, far_set), full_far, preferred_element_type=jnp.float32)
        combined = combined.astype(jnp.bfloat16)
        if term_index < TERMS:
            sent = combined.T
            got = lax.all_to_all(sent, ("row", "hi"), split_axis=0, concat_axis=0, tiled=True)
            got = got.reshape(2 * shard_count, half, 2, half)
            flipped = jnp.transpose(got, (2, 1, 0, 3)).reshape(row_count, state_count)
            increment = -(combined.astype(jnp.float32) + flipped.astype(jnp.float32)) / term_index
            running = running + increment
            current = increment.astype(jnp.bfloat16)
    running = running - combined.astype(jnp.float32) / TERMS
    leaving = lax.dynamic_slice_in_dim(running, (1 - hi) * half, half, 0).astype(jnp.bfloat16)
    staying = lax.dynamic_slice_in_dim(running, hi * half, half, 0)
    landed = swapped(leaving).astype(jnp.float32)
    blocks = combined.reshape(2, half, shard_count, row_count)
    blocks = jnp.transpose(blocks, (0, 2, 3, 1)).reshape(2 * state_count, half)
    got = lax.all_to_all(blocks, ("hi", "row"), split_axis=0, concat_axis=0, tiled=True)
    got = got.reshape(2, shard_count, row_count, half)
    flipped = jnp.transpose(got, (2, 1, 0, 3)).reshape(row_count, state_count)
    rows = jnp.concatenate([jnp.where(first, staying, landed), jnp.where(first, landed, staying)])
    return (own_ham.astype(jnp.float32) + rows - flipped.astype(jnp.float32) / TERMS)[None]


def solution(mesh):
    chans, rows = mesh.devices.shape
    pairs = Mesh(mesh.devices.reshape(2, chans // 2, rows), ("hi", "lo", "row"))
    chan = ("hi", "lo")
    placed = (
        P(chan, "row", None),
        P(chan, "row", None),
        P(chan),
        P(chan, None),
        P(chan, None),
        P(chan, None),
        P(),
    )
    return jax.shard_map(
        on_device, mesh=pairs, in_specs=placed, out_specs=P(chan, "row", None), check_vma=False
    )
```

profile of v0, /device:TPU:0, one launch (start us, length us, event | category | flops | bytes accessed | tf_op | source)
XLA Modules:
  0.0 352.6 jit_solution(11028163509748805113)
XLA Ops:
  7.2 2.8 and_select_fusion.1
  10.1 3.2 collective-permute-start.2
  13.3 18.5 %collective-permute-done.2 = bf16[160,2560]{1,0:T(8,128)(2,1)S(1)} collective-permute-done((bf16[160,2560]{1,0:T(8,128)(2,1)}, bf16[160,2560]{1,0:T(8,128)(2,1)S(1)}, u32[]{:S(2)}, u32[]{:S(2)}) %collective-permute-start.2) | collective-permute-done | bytes 819232 | tf_op jit(solution)/shard_map/ppermute | solution.py:10
  32.7 9.9 %scatter_custom_fusion = s32[2560]{0:T(1024)S(1)} fusion(s32[2560]{0:T(1024)S(1)} %fusion.31, s32[2560]{0:T(1024)S(1)} %reduce.1, s32[]{:T(128)} %constant.13.clone.1), kind=kCustom, calls=%fused_computation.88 | custom fusion | bytes 10244 | tf_op jit(solution)/shard_map/scatter | solution.py:36
  42.8 3.3 collective-permute-start.1
  58.6 46.6 %all-gather.3.cloned.1.call-done = bf16[2560,2560]{1,0:T(8,128)(2,1)} async-done(((bf16[160,2560]{1,0:T(8,128)(2,1)}), bf16[2560,2560]{1,0:T(8,128)(2,1)}) %all-gather.3.cloned.1.call-update) | async-done | bytes 13107216 | tf_op jit(solution)/shard_map/all_gather | solution.py:33
  105.2 8.2 %fusion.10 = f32[160,2560]{1,0:T(8,128)} fusion(bf16[2560,2560]{1,0:T(8,128)(2,1)} %all-gather.3.cloned.1.call-done, bf16[80,2560]{1,0:T(8,128)(2,1)S(1)} %get-tuple-element.26, bf16[80,2560]{1,0:T(8,128)(2,1)S(1)} %get-tuple-element.25), kind=kOutput, calls=%fused_computation.26 | convolution fusion | flops 2098790400 | bytes 15564800 | tf_op jit(solution)/shard_map/dot_general | solution.py:65
  113.4 86.2 %all-gather.5.cloned.1.call-done = bf16[2560,2560]{1,0:T(8,128)(2,1)} async-done(((bf16[160,2560]{1,0:T(8,128)(2,1)}), bf16[2560,2560]{1,0:T(8,128)(2,1)}) %all-gather.5.cloned.1.call-update) | async-done | bytes 13107216 | tf_op jit(solution)/shard_map/all_gather | solution.py:34
  199.6 7.5 %fusion = bf16[160,2560]{1,0:T(8,128)(2,1)S(1)} fusion(f32[160,2560]{1,0:T(8,128)} %fusion.10, bf16[2560,2560]{1,0:T(8,128)(2,1)} %all-gather.5.cloned.1.call-done, bf16[80,2560]{1,0:T(8,128)(2,1)S(1)} %get-tuple-element.24, bf16[80,2560]{1,0:T(8,128)(2,1)S(1)} %get-tuple-element.23), kind=kOutput, calls=%fused_computation.4 | convolution fusion | flops 2099609600 | bytes 16384000 | tf_op jit(solution)/shard_map/dot_general | solution.py:67
  207.1 1.6 all_to_all.18
  209.3 29.8 %all_to_all.27 = bf16[32,80,160]{1,2,0:T(8,128)(2,1)S(1)} all-to-all(bf16[32,80,160]{1,2,0:T(8,128)(2,1)S(1)} %copy.14), channel_id=1, replica_groups=mesh['hi'=2,'lo'=4,'row'=16] {'row','hi'}, dimensions={0} | all-to-all | bytes 1638400 | tf_op jit(solution)/shard_map/all_to_all | solution.py:71
  239.1 2.7 copy.15
  241.7 2.9 reshape.143
  245.3 7.3 %fusion.17 = f32[160,2560]{1,0:T(8,128)S(1)} fusion(bf16[2560,2560]{1,0:T(8,128)(2,1)} %all-gather.3.cloned.1.call-done, bf16[80,2560]{1,0:T(8,128)(2,1)S(1)} %get-tuple-element.22, bf16[80,2560]{1,0:T(8,128)(2,1)S(1)} %get-tuple-element.21), kind=kOutput, calls=%fused_computation.33 | convolution fusion | flops 2098790400 | bytes 15564800 | tf_op jit(solution)/shard_map/dot_general | solution.py:65
  253.2 2.3 fusion.1
  255.5 2.4 all_to_all.20
  258.0 1.8 copy.16
  259.8 24.2 %all_to_all.28 = bf16[32,80,160]{1,2,0:T(8,128)(2,1)S(1)} all-to-all(bf16[32,80,160]{1,2,0:T(8,128)(2,1)S(1)} %copy.16), channel_id=1, replica_groups=mesh['hi'=2,'lo'=4,'row'=16] {'row','hi'}, dimensions={0} | all-to-all | bytes 1638400 | tf_op jit(solution)/shard_map/all_to_all | solution.py:71
  284.0 1.8 convert_bitcast_fusion
  285.8 4.3 %copy.17 = f32[2,80,32,80]{3,2,1,0:T(8,128)} copy(f32[2,80,32,80]{1,3,0,2:T(8,128)} %convert_bitcast_fusion) | data formatting | bytes 3276800 | tf_op jit(solution)/shard_map/convert_element_type | solution.py:74
  290.1 2.9 reshape.144
  293.1 1.5 fusion.6
  295.0 7.2 %fusion.24 = f32[160,2560]{1,0:T(8,128)S(1)} fusion(bf16[2560,2560]{1,0:T(8,128)(2,1)} %all-gather.3.cloned.1.call-done, bf16[80,2560]{1,0:T(8,128)(2,1)S(1)} %get-tuple-element.18, bf16[80,2560]{1,0:T(8,128)(2,1)S(1)} %get-tuple-element.17), kind=kOutput, calls=%fused_computation.40 | convolution fusion | flops 2098790400 | bytes 15564800 | tf_op jit(solution)/shard_map/dot_general | solution.py:65
  302.4 3.5 multiply_subtract_fusion
  307.0 2.6 reshape.142
  309.6 2.3 copy.18
  311.9 6.0 %all-to-all-start.2 = ((bf16[32,160,80]{2,1,0:T(8,128)(2,1)}), bf16[32,160,80]{2,1,0:T(8,128)(2,1)S(1)}, u32[]{:S(2)}, u32[]{:S(2)}) async-start(bf16[32,160,80]{2,1,0:T(8,128)(2,1)} %bitcast.17), calls=%async_computation.2 | async-start | bytes 2621440 | tf_op jit(solution)/shard_map/all_to_all | solution.py:83
  317.9 2.4 fusion.7
  320.3 14.9 %all-to-all-done.2 = bf16[32,160,80]{2,1,0:T(8,128)(2,1)S(1)} async-done(((bf16[32,160,80]{2,1,0:T(8,128)(2,1)}), bf16[32,160,80]{2,1,0:T(8,128)(2,1)S(1)}, u32[]{:S(2)}, u32[]{:S(2)}) %all-to-all-start.2) | async-done | bytes 819232 | tf_op jit(solution)/shard_map/all_to_all | solution.py:83
  335.5 2.0 copy.19
  337.6 4.7 %div.26 = f32[1,160,2560]{2,1,0:T(8,128)} reshape(f32[160,16,2,80]{3,2,1,0:T(2,128)S(1)} %copy.19) | data formatting | bytes 3276800 | tf_op jit(solution)/shard_map/div | solution.py:87
  342.3 3.5 fusion.3
  (76 shorter events, 7.3 us)
Async XLA Ops:
  6.5 98.7 %all-gather.3.cloned.1.call-start = ((), (), s32[]{:S(2)}) async-start(), calls=%async_computation.3 | async-start | bytes 13926400 | tf_op jit(solution)/shard_map/all_gather | solution.py:33
  10.0 22.7 %copy-start.8 = (s32[1,2560]{1,0:T(1,128)S(1)}, s32[1,2560]{1,0:T(1,128)}, u32[]{:S(2)}) copy-start(s32[1,2560]{1,0:T(1,128)} %param.11) | copy-start | bytes 30724
  10.0 22.7 %copy-start.9 = (s32[1,2560]{1,0:T(1,128)S(1)}, s32[1,2560]{1,0:T(1,128)}, u32[]{:S(2)}) copy-start(s32[1,2560]{1,0:T(1,128)} %param.12) | copy-start | bytes 30724
  10.0 32.7 %copy-start.10 = (s32[1,2560]{1,0:T(1,128)S(1)}, s32[1,2560]{1,0:T(1,128)}, u32[]{:S(2)}) copy-start(s32[1,2560]{1,0:T(1,128)} %param.10) | copy-start | bytes 30724
  10.0 36.5 %copy-start.11 = (f32[8,2]{0,1:T(2,128)S(1)}, f32[8,2]{0,1:T(2,128)}, u32[]{:S(2)}) copy-start(f32[8,2]{0,1:T(2,128)} %param.13) | copy-start | bytes 196
  10.0 189.6 %all-gather.5.cloned.1.call-start = ((), (), s32[]{:S(2)}) async-start(), calls=%async_computation.4 | async-start | bytes 13926400 | tf_op jit(solution)/shard_map/all_gather | solution.py:34
  10.1 21.7 %collective-permute-start.2 = (bf16[160,2560]{1,0:T(8,128)(2,1)}, bf16[160,2560]{1,0:T(8,128)(2,1)S(1)}, u32[]{:S(2)}, u32[]{:S(2)}) collective-permute-start(bf16[160,2560]{1,0:T(8,128)(2,1)} %get-tuple-element.38), channel_id=1, source_target_pairs={{0,64},{64,0},{1,65},{65,1},{2,66},{66,2},{3,67},{67,3},{4,68},{68... | collective-permute-start | bytes 2457608 | tf_op jit(solution)/shard_map/ppermute | solution.py:10
  31.7 0.9 copy-start.7
  42.8 14.3 %collective-permute-start.1 = (f32[2,2560]{1,0:T(2,128)S(1)}, f32[2,2560]{1,0:T(2,128)S(1)}, u32[]{:S(2)}, u32[]{:S(2)}) collective-permute-start(f32[2,2560]{1,0:T(2,128)S(1)} %add_convert_fusion.12), channel_id=1, source_target_pairs={{0,64},{64,0},{1,65},{65,1},{2,66},{66,2},{3,67},{67,3},{4,68},{68... | collective-permute-start | bytes 61448 | tf_op jit(solution)/shard_map/ppermute | solution.py:10
  46.1 11.8 %collective-permute-start = (bf16[80,2560]{1,0:T(8,128)(2,1)S(1)}, bf16[80,2560]{1,0:T(8,128)(2,1)S(1)}, u32[]{:S(2)}, u32[]{:S(2)}) collective-permute-start(bf16[80,2560]{1,0:T(8,128)(2,1)S(1)} %constant_dynamic-slice_fusion.2), channel_id=1, source_target_pairs={{0,64},{64,0},{1,65},{65,1},{2,66},{66,2},{3,67},{67,3},{4,68},{68... | collective-permute-start | bytes 1228808 | tf_op jit(solution)/shard_map/ppermute | solution.py:10
  207.1 37.5 %copy-start = (bf16[160,2560]{1,0:T(8,128)(2,1)}, bf16[160,2560]{1,0:T(8,128)(2,1)S(1)}, u32[]{:S(2)}) copy-start(bf16[160,2560]{1,0:T(8,128)(2,1)S(1)} %fusion) | copy-start | bytes 2457604
  244.7 8.0 %slice-start = ((s8[13107200]{0:T(1024)(128)(4,1)}), s8[4194304]{0:T(1024)(128)(4,1)S(1)}, s32[]{:S(2)}) async-start(s8[13107200]{0:T(1024)(128)(4,1)} %bitcast.49), calls=%async_computation.5 | async-start | bytes 8388608
  244.9 7.8 %slice-start.1 = ((s8[13107200]{0:T(1024)(128)(4,1)}), s8[4194304]{0:T(1024)(128)(4,1)S(1)}, s32[]{:S(2)}) async-start(s8[13107200]{0:T(1024)(128)(4,1)} %bitcast.49), calls=%async_computation.6 | async-start | bytes 8388608
  245.3 7.9 %slice-start.2 = ((s8[13107200]{0:T(1024)(128)(4,1)}), s8[4194304]{0:T(1024)(128)(4,1)S(1)}, s32[]{:S(2)}) async-start(s8[13107200]{0:T(1024)(128)(4,1)} %bitcast.49), calls=%async_computation.7 | async-start | bytes 8388608
  245.3 7.9 %slice-start.3 = ((s8[13107200]{0:T(1024)(128)(4,1)}), s8[524288]{0:T(1024)(128)(4,1)S(1)}, s32[]{:S(2)}) async-start(s8[13107200]{0:T(1024)(128)(4,1)} %bitcast.49), calls=%async_computation.8 | async-start | bytes 1048576
  255.5 4.3 %copy-start.2 = (bf16[160,2560]{1,0:T(8,128)(2,1)}, bf16[160,2560]{1,0:T(8,128)(2,1)S(1)}, u32[]{:S(2)}) copy-start(bf16[160,2560]{1,0:T(8,128)(2,1)S(1)} %fusion.1) | copy-start | bytes 2457604
  293.0 9.2 %slice-start.4 = ((s8[13107200]{0:T(1024)(128)(4,1)}), s8[4194304]{0:T(1024)(128)(4,1)S(1)}, s32[]{:S(2)}) async-start(s8[13107200]{0:T(1024)(128)(4,1)} %bitcast.51), calls=%async_computation.9 | async-start | bytes 8388608
  294.6 7.7 %slice-start.5 = ((s8[13107200]{0:T(1024)(128)(4,1)}), s8[4194304]{0:T(1024)(128)(4,1)S(1)}, s32[]{:S(2)}) async-start(s8[13107200]{0:T(1024)(128)(4,1)} %bitcast.51), calls=%async_computation.10 | async-start | bytes 8388608
  295.0 7.3 %slice-start.6 = ((s8[13107200]{0:T(1024)(128)(4,1)}), s8[4194304]{0:T(1024)(128)(4,1)S(1)}, s32[]{:S(2)}) async-start(s8[13107200]{0:T(1024)(128)(4,1)} %bitcast.51), calls=%async_computation.11 | async-start | bytes 8388608
  295.0 7.3 %slice-start.7 = ((s8[13107200]{0:T(1024)(128)(4,1)}), s8[524288]{0:T(1024)(128)(4,1)S(1)}, s32[]{:S(2)}) async-start(s8[13107200]{0:T(1024)(128)(4,1)} %bitcast.51), calls=%async_computation.12 | async-start | bytes 1048576
  295.0 7.3 %copy-start.1 = (bf16[160,2560]{1,0:T(8,128)(2,1)S(1)}, bf16[160,2560]{1,0:T(8,128)(2,1)}, u32[]{:S(2)}) copy-start(bf16[160,2560]{1,0:T(8,128)(2,1)} %copy-done) | copy-start | bytes 2457604
  295.0 7.4 %copy-start.3 = (bf16[160,2560]{1,0:T(8,128)(2,1)S(1)}, bf16[160,2560]{1,0:T(8,128)(2,1)}, u32[]{:S(2)}) copy-start(bf16[160,2560]{1,0:T(8,128)(2,1)} %copy-done.2) | copy-start | bytes 2457604
  305.9 1.2 copy-start.4
  305.9 12.0 %collective-permute-start.3 = (bf16[80,2560]{1,0:T(8,128)(2,1)S(1)}, bf16[80,2560]{1,0:T(8,128)(2,1)}, u32[]{:S(2)}, u32[]{:S(2)}) collective-permute-start(bf16[80,2560]{1,0:T(8,128)(2,1)S(1)} %dynamic-slice_convert_fusion), channel_id=1, source_target_pairs={{0,64},{64,0},{1,65},{65,1},{2,66},{66,2},{3,67},{67,3},{4,68},{68... | collective-permute-start | bytes 1228808 | tf_op jit(solution)/shard_map/ppermute | solution.py:10
  311.9 6.0 %copy-start.5 = (f32[160,2560]{1,0:T(8,128)S(1)}, f32[160,2560]{1,0:T(8,128)}, u32[]{:S(2)}) copy-start(f32[160,2560]{1,0:T(8,128)} %copy-done.4) | copy-start | bytes 4915204
  311.9 23.3 %all-to-all-start.2 = ((bf16[32,160,80]{2,1,0:T(8,128)(2,1)}), bf16[32,160,80]{2,1,0:T(8,128)(2,1)S(1)}, u32[]{:S(2)}, u32[]{:S(2)}) async-start(bf16[32,160,80]{2,1,0:T(8,128)(2,1)} %bitcast.17), calls=%async_computation.2 | async-start | bytes 2621440 | tf_op jit(solution)/shard_map/all_to_all | solution.py:83
  337.6 4.7 %copy-start.6 = (bf16[1,160,2560]{2,1,0:T(8,128)(2,1)S(1)}, bf16[1,160,2560]{2,1,0:T(8,128)(2,1)}, u32[]{:S(2)}) copy-start(bf16[1,160,2560]{2,1,0:T(8,128)(2,1)} %param.8) | copy-start | bytes 2457604
Sparse Core Ops, SparseCore 0:
  10.1 95.0 all-gather.2
  107.4 92.1 all-gather.4
where the time goes:
time: 353 us
  waiting for transfers between devices  167 us (47%)
  blocking collectives  54 us (15%)
  local copies, waits for them, and re-layouts  43.7 us (12%)
  matrix products  36 us (10%)
  between operations  24.5 us (7%)
  other arithmetic  14.2 us (4%)
  starting transfers between devices  13.6 us (4%)
    all_gather x1, waiting for transfers between devices, on_device(): full_far = lax.all_gather(far_share, 'row', axis=0, tiled=True)  86.2 us
    all_to_all x2, blocking collectives, on_device(): lax.all_to_all(sent, ('row', 'hi'), split_axis=0, concat_axis=0, tiled=True)  54 us
    all_gather x1, waiting for transfers between devices, on_device(): full_own = lax.all_gather(own_share, 'row', axis=0, tiled=True)  46.6 us
    dot_general x3, matrix products, on_device(): jnp.dot(mix(wide, own_set), full_own, preferred_element_type=jnp.float32)  22.7 us
    ppermute x4, waiting for transfers between devices, swapped(): return lax.ppermute(value, 'hi', [(0, 1), (1, 0)])  18.8 us
    all_to_all x1, waiting for transfers between devices, on_device(): lax.all_to_all(blocks, ('hi', 'row'), split_axis=0, concat_axis=0, tiled=...  14.9 us
    dot_general x3, matrix products, on_device(): jnp.dot(mix(wide, far_set), full_far, preferred_element_type=jnp.float32)  13.3 us
    convert_element_type x4, local copies, waits for them, and re-layouts, on_device(): flipped.astype(jnp.float32)  12.8 us
  transfers between devices with their start and end apart: 7, of which 5 were waited for; matrix products, arithmetic and copies ran while one was open for 8% of the time, Pallas kernels for 0%

commit v1 on v0

--- a/solution.py
+++ b/solution.py
@@ -31,7 +31,10 @@
     own_share = jnp.where(block_alive, generator[0], jnp.zeros_like(generator[0]))
     far_share = swapped(own_share)
     full_own = lax.all_gather(own_share, "row", axis=0, tiled=True)
-    full_far = lax.all_gather(far_share, "row", axis=0, tiled=True)
+    size = lax.axis_size("row")
+    parts = jnp.stack([far_share for _ in range(size)])
+    parts = lax.all_to_all(parts, "row", split_axis=0, concat_axis=0)
+    full_far = jnp.concatenate(parts, axis=0)
     pp = jnp.where(column_alive, pp_occupation[0], 0)
     ph = jnp.zeros((state_count,), jnp.int32).at[ph_order[0]].set(ph_occupation[0])
     ph = jnp.where(column_alive, ph, 0)

time: 353 us -> 470 us (1.33)
  waiting for transfers between devices: 167 us -> 260 us
  matrix products: 36 us -> 45.1 us
  starting transfers between devices: 13.6 us -> 22 us
    all_gather x1, waiting for transfers between devices: 46.6 us -> 176 us  [on_device(): full_own = lax.all_gather(own_share, 'row', axis=0, tiled=True)]
    all_gather x1 -> x0, waiting for transfers between devices: 86.2 us -> none  [on_device(): full_far = lax.all_gather(far_share, 'row', axis=0, tiled=True)]
    all_to_all x0 -> x1, waiting for transfers between devices: none -> 51.8 us  [on_device(): parts = lax.all_to_all(parts, 'row', split_axis=0, concat_axis=0)]
    dot_general x3, matrix products: 13.3 us -> 22.8 us  [on_device(): jnp.dot(mix(wide, far_set), full_far, preferred_element_type=jnp.float32)]
    all_to_all x0 -> x1, starting transfers between devices: none -> 8.46 us  [on_device(): parts = lax.all_to_all(parts, 'row', split_axis=0, concat_axis=0)]
    another operation x0 -> x1, local copies, waits for them, and re-layouts: none -> 5.98 us  [on_device(): parts = jnp.stack([far_share for _ in range(size)])]
  transfers between devices with their start and end apart: 7 -> 7, of which waited for: 5 -> 4; matrix products, arithmetic and copies ran while one was open for 8% -> 7% of each run, Pallas kernels for 0% -> 0%
where the time goes in v1:
time: 470 us; the launch traced here: 469 us
  waiting for transfers between devices  260 us (55%)
  blocking collectives  55.1 us (12%)
  local copies, waits for them, and re-layouts  48.2 us (10%)
  matrix products  45.1 us (10%)
  between operations  24.3 us (5%)
  starting transfers between devices  22 us (5%)
  other arithmetic  14 us (3%)
    all_gather x1, waiting for transfers between devices, on_device(): full_own = lax.all_gather(own_share, 'row', axis=0, tiled=True)  176 us
    all_to_all x2, blocking collectives, on_device(): lax.all_to_all(sent, ('row', 'hi'), split_axis=0, concat_axis=0, tiled=True)  55.1 us
    all_to_all x1, waiting for transfers between devices, on_device(): parts = lax.all_to_all(parts, 'row', split_axis=0, concat_axis=0)  51.8 us
    dot_general x3, matrix products, on_device(): jnp.dot(mix(wide, far_set), full_far, preferred_element_type=jnp.float32)  22.8 us
    dot_general x3, matrix products, on_device(): jnp.dot(mix(wide, own_set), full_own, preferred_element_type=jnp.float32)  22.3 us
    ppermute x4, waiting for transfers between devices, swapped(): return lax.ppermute(value, 'hi', [(0, 1), (1, 0)])  18.5 us
    all_to_all x1, waiting for transfers between devices, on_device(): lax.all_to_all(blocks, ('hi', 'row'), split_axis=0, concat_axis=0, tiled=...  13.7 us
    convert_element_type x4, local copies, waits for them, and re-layouts, on_device(): flipped.astype(jnp.float32)  12.8 us
  transfers between devices with their start and end apart: 7, of which 4 were waited for; matrix products, arithmetic and copies ran while one was open for 7% of the time, Pallas kernels for 0%

profile of v1, /device:TPU:0, one launch (start us, length us, event | category | flops | bytes accessed | tf_op | source)
XLA Modules:
  0.0 469.0 jit_solution(8768343203140598625)
XLA Ops:
  7.2 2.8 and_select_fusion.1
  10.0 3.2 collective-permute-start.2
  13.2 18.5 %collective-permute-done.2 = bf16[160,2560]{1,0:T(8,128)(2,1)S(1)} collective-permute-done((bf16[160,2560]{1,0:T(8,128)(2,1)}, bf16[160,2560]{1,0:T(8,128)(2,1)S(1)}, u32[]{:S(2)}, u32[]{:S(2)}) %collective-permute-start.2) | collective-permute-done | bytes 819232 | tf_op jit(solution)/shard_map/ppermute | solution.py:10
  31.7 6.0 %stack.14 = bf16[16,160,2560]{2,1,0:T(8,128)(2,1)} broadcast(bf16[160,2560]{1,0:T(8,128)(2,1)S(1)} %collective-permute-done.2), dimensions={1,2} | broadcast | bytes 13926400 | tf_op jit(solution)/shard_map/stack | solution.py:35
  37.7 8.5 %all-to-all-start = ((bf16[16,160,2560]{2,1,0:T(8,128)(2,1)}), bf16[16,160,2560]{2,1,0:T(8,128)(2,1)}, u32[]{:S(2)}, u32[]{:S(2)}) async-start(bf16[16,160,2560]{2,1,0:T(8,128)(2,1)} %stack.14), calls=%async_computation | async-start | bytes 26214400 | tf_op jit(solution)/shard_map/all_to_all | solution.py:36
  46.2 9.9 %scatter_custom_fusion = s32[2560]{0:T(1024)S(1)} fusion(s32[2560]{0:T(1024)S(1)} %fusion.31, s32[2560]{0:T(1024)S(1)} %reduce.1, s32[]{:T(128)} %constant.13.clone.1), kind=kCustom, calls=%fused_computation.88 | custom fusion | bytes 10244 | tf_op jit(solution)/shard_map/scatter | solution.py:39
  56.3 3.1 collective-permute-start.1
  71.7 176.4 %all-gather.2.cloned.1.call-done = bf16[2560,2560]{1,0:T(8,128)(2,1)} async-done(((bf16[160,2560]{1,0:T(8,128)(2,1)}), bf16[2560,2560]{1,0:T(8,128)(2,1)}) %all-gather.2.cloned.1.call-update) | async-done | bytes 13107216 | tf_op jit(solution)/shard_map/all_gather | solution.py:33
  248.1 8.2 %fusion.10 = f32[160,2560]{1,0:T(8,128)} fusion(bf16[2560,2560]{1,0:T(8,128)(2,1)} %all-gather.2.cloned.1.call-done, bf16[80,2560]{1,0:T(8,128)(2,1)S(1)} %get-tuple-element.26, bf16[80,2560]{1,0:T(8,128)(2,1)S(1)} %get-tuple-element.25), kind=kOutput, calls=%fused_computation.26 | convolution fusion | flops 2098790400 | bytes 15564800 | tf_op jit(solution)/shard_map/dot_general | solution.py:68
  256.3 51.8 %all-to-all-done = bf16[16,160,2560]{2,1,0:T(8,128)(2,1)} async-done(((bf16[16,160,2560]{2,1,0:T(8,128)(2,1)}), bf16[16,160,2560]{2,1,0:T(8,128)(2,1)}, u32[]{:S(2)}, u32[]{:S(2)}) %all-to-all-start) | async-done | bytes 13107232 | tf_op jit(solution)/shard_map/all_to_all | solution.py:36
  308.1 7.4 %fusion = bf16[160,2560]{1,0:T(8,128)(2,1)S(1)} fusion(f32[160,2560]{1,0:T(8,128)} %fusion.10, bf16[2560,2560]{1,0:T(8,128)(2,1)} %bitcast.8, bf16[80,2560]{1,0:T(8,128)(2,1)S(1)} %get-tuple-element.24, bf16[80,2560]{1,0:T(8,128)(2,1)S(1)} %get-tuple-element.23), kind=kOutput, calls=%fused_computation.4 | convolution fusion | flops 2099609600 | bytes 16384000 | tf_op jit(solution)/shard_map/dot_general | solution.py:70
  317.7 31.8 %all_to_all.32 = bf16[32,80,160]{1,2,0:T(8,128)(2,1)S(1)} all-to-all(bf16[32,80,160]{1,2,0:T(8,128)(2,1)S(1)} %copy.14), channel_id=1, replica_groups=mesh['hi'=2,'lo'=4,'row'=16] {'row','hi'}, dimensions={0} | all-to-all | bytes 1638400 | tf_op jit(solution)/shard_map/all_to_all | solution.py:74
  349.5 2.7 copy.15
  352.2 2.9 reshape.149
  355.7 7.0 %fusion.17 = f32[160,2560]{1,0:T(8,128)S(1)} fusion(bf16[2560,2560]{1,0:T(8,128)(2,1)} %all-gather.2.cloned.1.call-done, bf16[80,2560]{1,0:T(8,128)(2,1)S(1)} %get-tuple-element.22, bf16[80,2560]{1,0:T(8,128)(2,1)S(1)} %get-tuple-element.21), kind=kOutput, calls=%fused_computation.33 | convolution fusion | flops 2098790400 | bytes 15564800 | tf_op jit(solution)/shard_map/dot_general | solution.py:68
  362.8 7.0 %fusion.1 = bf16[160,2560]{1,0:T(8,128)(2,1)S(1)} fusion(f32[160,2560]{1,0:T(8,128)S(1)} %fusion.17, bf16[2560,2560]{1,0:T(8,128)(2,1)} %bitcast.8, bf16[80,2560]{1,0:T(8,128)(2,1)S(1)} %get-tuple-element.20, bf16[80,2560]{1,0:T(8,128)(2,1)S(1)} %get-tuple-element.19), kind=kOutput, calls=%fused_computation.5 | convolution fusion | flops 2099609600 | bytes 16384000 | tf_op jit(solution)/shard_map/dot_general | solution.py:70
  369.8 2.4 all_to_all.24
  372.2 1.8 copy.16
  374.1 23.2 %all_to_all.33 = bf16[32,80,160]{1,2,0:T(8,128)(2,1)S(1)} all-to-all(bf16[32,80,160]{1,2,0:T(8,128)(2,1)S(1)} %copy.16), channel_id=1, replica_groups=mesh['hi'=2,'lo'=4,'row'=16] {'row','hi'}, dimensions={0} | all-to-all | bytes 1638400 | tf_op jit(solution)/shard_map/all_to_all | solution.py:74
  397.3 1.8 convert_bitcast_fusion
  399.1 4.3 copy.17
  403.4 2.9 reshape.150
  408.1 7.1 %fusion.24 = f32[160,2560]{1,0:T(8,128)S(1)} fusion(bf16[2560,2560]{1,0:T(8,128)(2,1)} %all-gather.2.cloned.1.call-done, bf16[80,2560]{1,0:T(8,128)(2,1)S(1)} %get-tuple-element.18, bf16[80,2560]{1,0:T(8,128)(2,1)S(1)} %get-tuple-element.17), kind=kOutput, calls=%fused_computation.40 | convolution fusion | flops 2098790400 | bytes 15564800 | tf_op jit(solution)/shard_map/dot_general | solution.py:68
  415.3 8.3 %multiply_subtract_fusion = (f32[160,2560]{1,0:T(8,128)S(1)}, bf16[160,2560]{1,0:T(8,128)(2,1)}) fusion(f32[160,2560]{1,0:T(8,128)S(1)} %reshape.149, bf16[160,2560]{1,0:T(8,128)(2,1)S(1)} %copy-done.1, f32[160,2560]{1,0:T(8,128)S(1)} %reshape.150, bf16[160,2560]{1,0:T(8,128)(2,1)S(1)} %copy-done.3, f32[160,2560]{1,0:T(8,128)S(1)} %fusion.24, ...), kind=kOutput, calls=%fused_computation.13 | convolution fusion | flops 2104115200 | bytes 22937600 | tf_op jit(solution)/shard_map/dot_general | solution.py:70
  424.8 2.6 reshape.148
  427.4 2.3 copy.18
  429.6 6.0 %all-to-all-start.3 = ((bf16[32,160,80]{2,1,0:T(8,128)(2,1)}), bf16[32,160,80]{2,1,0:T(8,128)(2,1)S(1)}, u32[]{:S(2)}, u32[]{:S(2)}) async-start(bf16[32,160,80]{2,1,0:T(8,128)(2,1)} %bitcast.18), calls=%async_computation.3 | async-start | bytes 2621440 | tf_op jit(solution)/shard_map/all_to_all | solution.py:86
  435.6 2.4 fusion.7
  438.0 13.7 %all-to-all-done.3 = bf16[32,160,80]{2,1,0:T(8,128)(2,1)S(1)} async-done(((bf16[32,160,80]{2,1,0:T(8,128)(2,1)}), bf16[32,160,80]{2,1,0:T(8,128)(2,1)S(1)}, u32[]{:S(2)}, u32[]{:S(2)}) %all-to-all-start.3) | async-done | bytes 819232 | tf_op jit(solution)/shard_map/all_to_all | solution.py:86
  452.0 2.0 copy.19
  454.0 4.7 %div.26 = f32[1,160,2560]{2,1,0:T(8,128)} reshape(f32[160,16,2,80]{3,2,1,0:T(2,128)S(1)} %copy.19) | data formatting | bytes 3276800 | tf_op jit(solution)/shard_map/div | solution.py:90
  458.7 3.5 fusion.3
  (56 shorter events, 8.5 us)
Async XLA Ops:
  6.5 241.6 %all-gather.2.cloned.1.call-start = ((), (), s32[]{:S(2)}) async-start(), calls=%async_computation.4 | async-start | bytes 13926400 | tf_op jit(solution)/shard_map/all_gather | solution.py:33
  10.0 21.7 %collective-permute-start.2 = (bf16[160,2560]{1,0:T(8,128)(2,1)}, bf16[160,2560]{1,0:T(8,128)(2,1)S(1)}, u32[]{:S(2)}, u32[]{:S(2)}) collective-permute-start(bf16[160,2560]{1,0:T(8,128)(2,1)} %get-tuple-element.38), channel_id=1, source_target_pairs={{0,64},{64,0},{1,65},{65,1},{2,66},{66,2},{3,67},{67,3},{4,68},{68... | collective-permute-start | bytes 2457608 | tf_op jit(solution)/shard_map/ppermute | solution.py:10
  37.7 8.5 %copy-start.7 = (s32[1,2560]{1,0:T(1,128)S(1)}, s32[1,2560]{1,0:T(1,128)}, u32[]{:S(2)}) copy-start(s32[1,2560]{1,0:T(1,128)} %param.11) | copy-start | bytes 30724
  37.7 8.5 %copy-start.8 = (s32[1,2560]{1,0:T(1,128)S(1)}, s32[1,2560]{1,0:T(1,128)}, u32[]{:S(2)}) copy-start(s32[1,2560]{1,0:T(1,128)} %param.12) | copy-start | bytes 30724
  37.7 18.5 %copy-start.9 = (s32[1,2560]{1,0:T(1,128)S(1)}, s32[1,2560]{1,0:T(1,128)}, u32[]{:S(2)}) copy-start(s32[1,2560]{1,0:T(1,128)} %param.10) | copy-start | bytes 30724
  37.7 22.3 %copy-start.10 = (f32[8,2]{0,1:T(2,128)S(1)}, f32[8,2]{0,1:T(2,128)}, u32[]{:S(2)}) copy-start(f32[8,2]{0,1:T(2,128)} %param.13) | copy-start | bytes 196
  37.7 270.4 %all-to-all-start = ((bf16[16,160,2560]{2,1,0:T(8,128)(2,1)}), bf16[16,160,2560]{2,1,0:T(8,128)(2,1)}, u32[]{:S(2)}, u32[]{:S(2)}) async-start(bf16[16,160,2560]{2,1,0:T(8,128)(2,1)} %stack.14), calls=%async_computation | async-start | bytes 26214400 | tf_op jit(solution)/shard_map/all_to_all | solution.py:36
  56.3 14.3 %collective-permute-start.1 = (f32[2,2560]{1,0:T(2,128)S(1)}, f32[2,2560]{1,0:T(2,128)S(1)}, u32[]{:S(2)}, u32[]{:S(2)}) collective-permute-start(f32[2,2560]{1,0:T(2,128)S(1)} %add_convert_fusion.12), channel_id=1, source_target_pairs={{0,64},{64,0},{1,65},{65,1},{2,66},{66,2},{3,67},{67,3},{4,68},{68... | collective-permute-start | bytes 61448 | tf_op jit(solution)/shard_map/ppermute | solution.py:10
  59.4 11.6 %collective-permute-start = (bf16[80,2560]{1,0:T(8,128)(2,1)S(1)}, bf16[80,2560]{1,0:T(8,128)(2,1)S(1)}, u32[]{:S(2)}, u32[]{:S(2)}) collective-permute-start(bf16[80,2560]{1,0:T(8,128)(2,1)S(1)} %constant_dynamic-slice_fusion.2), channel_id=1, source_target_pairs={{0,64},{64,0},{1,65},{65,1},{2,66},{66,2},{3,67},{67,3},{4,68},{68... | collective-permute-start | bytes 1228808 | tf_op jit(solution)/shard_map/ppermute | solution.py:10
  315.5 39.6 %copy-start = (bf16[160,2560]{1,0:T(8,128)(2,1)}, bf16[160,2560]{1,0:T(8,128)(2,1)S(1)}, u32[]{:S(2)}) copy-start(bf16[160,2560]{1,0:T(8,128)(2,1)S(1)} %fusion) | copy-start | bytes 2457604
  369.8 4.3 copy-start.2
  408.1 7.2 %copy-start.1 = (bf16[160,2560]{1,0:T(8,128)(2,1)S(1)}, bf16[160,2560]{1,0:T(8,128)(2,1)}, u32[]{:S(2)}) copy-start(bf16[160,2560]{1,0:T(8,128)(2,1)} %copy-done) | copy-start | bytes 2457604
  408.1 7.2 %copy-start.3 = (bf16[160,2560]{1,0:T(8,128)(2,1)S(1)}, bf16[160,2560]{1,0:T(8,128)(2,1)}, u32[]{:S(2)}) copy-start(bf16[160,2560]{1,0:T(8,128)(2,1)} %copy-done.2) | copy-start | bytes 2457604
  423.6 1.2 copy-start.4
  423.6 12.0 %collective-permute-start.3 = (bf16[80,2560]{1,0:T(8,128)(2,1)S(1)}, bf16[80,2560]{1,0:T(8,128)(2,1)}, u32[]{:S(2)}, u32[]{:S(2)}) collective-permute-start(bf16[80,2560]{1,0:T(8,128)(2,1)S(1)} %dynamic-slice_convert_fusion), channel_id=1, source_target_pairs={{0,64},{64,0},{1,65},{65,1},{2,66},{66,2},{3,67},{67,3},{4,68},{68... | collective-permute-start | bytes 1228808 | tf_op jit(solution)/shard_map/ppermute | solution.py:10
  429.6 6.0 %copy-start.5 = (f32[160,2560]{1,0:T(8,128)S(1)}, f32[160,2560]{1,0:T(8,128)}, u32[]{:S(2)}) copy-start(f32[160,2560]{1,0:T(8,128)} %copy-done.4) | copy-start | bytes 4915204
  429.6 22.0 %all-to-all-start.3 = ((bf16[32,160,80]{2,1,0:T(8,128)(2,1)}), bf16[32,160,80]{2,1,0:T(8,128)(2,1)S(1)}, u32[]{:S(2)}, u32[]{:S(2)}) async-start(bf16[32,160,80]{2,1,0:T(8,128)(2,1)} %bitcast.18), calls=%async_computation.3 | async-start | bytes 2621440 | tf_op jit(solution)/shard_map/all_to_all | solution.py:86
  454.0 4.7 %copy-start.6 = (bf16[1,160,2560]{2,1,0:T(8,128)(2,1)S(1)}, bf16[1,160,2560]{2,1,0:T(8,128)(2,1)}, u32[]{:S(2)}) copy-start(bf16[1,160,2560]{2,1,0:T(8,128)(2,1)} %param.8) | copy-start | bytes 2457604
Sparse Core Ops, SparseCore 0:
  10.1 237.9 all-gather.1
